TPU v7x, 512 devices: a whole 4x4x16 slice. The times are simulated.
512 devices in a mesh: dp: 16 (over z), ctx: 32 (over x, y, core).
Axes of the slice: x: 4, y: 4, z: 16, core: 2. Of those that a mesh axis runs over, the one named last changes fastest.
Arguments:
- tokens: bfloat16 [16, 8192, 1024], P('dp', 'ctx'), may hold values from -14 to 14
- w_query: bfloat16 [1024, 1024], replicated, may hold values from -0.1875 to 0.1875
- key_weight: bfloat16 [1024, 256], replicated, may hold values from -0.1875 to 0.1875
- value_weight: bfloat16 [1024, 256], replicated, may hold values from -0.1875 to 0.1875
- cotangent: bfloat16 [16, 8192, 1024], P('dp', 'ctx'), may hold values from -6 to 6
- segment_ids: int32 [16, 8192], P('dp'), may hold values from 0 to 3, never falling along the last dimension, each value on 1 to 4096 neighbouring positions
Outputs:
- grad_inputs: bfloat16 [16, 8192, 1024], P('dp', 'ctx')
- grad_query: float32 [1024, 1024], P('ctx')
- key_weight_gradient: float32 [1024, 256], P('ctx')
- value_weight_gradient: float32 [1024, 256], P('ctx')
Inputs may be any that keep to these rules, and one draw needn't show every extreme that they name: `segment_ids`: along each sequence the document numbers never fall and start at 0; each document has 1 to min(4096, 6144) bytes, and one has exactly that many.
All inputs are finite; a program needn't handle non-finite values.
Results may differ from a plain program's by a relative error of at most 0.014.
The roundings to bfloat16 on the way count: a program that leaves them out, or rounds other values in their place, can miss the bound.
Values may be sent and summed in bfloat16 or wider, within the bound.
A program may use at most 64 MiB of HBM per device.

v0:
```python
import jax
import jax.numpy as jnp
from jax import lax
from jax.sharding import PartitionSpec as P

HEAD_DIMENSION = 128
WINDOW = 1024
NEG_FILL = -1e30


def shifted(block, axis, distance):
    devices = range(lax.axis_size(axis))
    route = [(i - distance, i) for i in devices if i - distance in devices]
    return lax.ppermute(block, axis, route)


def head_terms(
    head_index, q_block, k_block, v_block, c_block, allowed, scale, head_size, group_size
):
    query_group = head_index // group_size
    query = lax.dynamic_slice_in_dim(q_block, head_index * head_size, head_size, 1)
    key_h = lax.dynamic_slice_in_dim(k_block, query_group * head_size, head_size, 1)
    value_h = lax.dynamic_slice_in_dim(v_block, query_group * head_size, head_size, 1)
    dout = lax.dynamic_slice_in_dim(c_block, head_index * head_size, head_size, 1)
    scores = jnp.dot(query, key_h.T, preferred_element_type=jnp.float32) * scale
    scores = jnp.where(allowed, scores, NEG_FILL)
    peak = jnp.max(scores, axis=1, keepdims=True)
    weights = jnp.exp(scores - peak)
    weights = weights / jnp.sum(weights, axis=1, keepdims=True)
    weights_b = weights.astype(jnp.bfloat16)
    attended = jnp.dot(weights_b, value_h, preferred_element_type=jnp.float32)
    delta = jnp.sum(dout.astype(jnp.float32) * attended, axis=1, keepdims=True)
    dprobs = jnp.dot(dout, value_h.T, preferred_element_type=jnp.float32)
    dscores = (weights * (dprobs - delta) * scale).astype(jnp.bfloat16)
    grad_q = jnp.dot(dscores, key_h, preferred_element_type=jnp.float32)
    key_gradient = jnp.dot(dscores.T, query, preferred_element_type=jnp.float32)
    value_gradient = jnp.dot(weights_b.T, dout, preferred_element_type=jnp.float32)
    return (grad_q, key_gradient, value_gradient)


def body(tokens, w_query, key_weight, value_weight, cotangent, segment_ids):
    sequence = tokens[0]
    cot = cotangent[0]
    seg = segment_ids[0]
    rows = sequence.shape[0]
    q_cols = w_query.shape[1]
    key_value_columns = key_weight.shape[1]
    head_size = HEAD_DIMENSION
    heads = q_cols // head_size
    kv_heads = key_value_columns // head_size
    group_size = heads // kv_heads
    reach = WINDOW // rows
    column_width = (reach + 1) * rows
    scale = head_size ** (-0.5)
    position = lax.axis_index("ctx")
    start = position * rows
    queries = jnp.dot(sequence, w_query, preferred_element_type=jnp.float32).astype(jnp.bfloat16)
    keys = jnp.dot(sequence, key_weight, preferred_element_type=jnp.float32).astype(jnp.bfloat16)
    values = jnp.dot(sequence, value_weight, preferred_element_type=jnp.float32).astype(
        jnp.bfloat16
    )
    earlier = [shifted((keys, values), "ctx", reach - slot) for slot in range(reach)]
    k_block = jnp.concatenate([pair[0] for pair in earlier] + [keys], axis=0)
    v_block = jnp.concatenate([pair[1] for pair in earlier] + [values], axis=0)
    seg_pad = jnp.concatenate([-jnp.ones((WINDOW,), jnp.int32), seg], axis=0)
    q_seg = lax.dynamic_slice_in_dim(seg, start, rows, 0)
    k_seg = lax.dynamic_slice_in_dim(seg_pad, start, column_width, 0)
    q_pos = start + jnp.arange(rows, dtype=jnp.int32)
    k_pos = start - reach * rows + jnp.arange(column_width, dtype=jnp.int32)
    gap = q_pos[:, None] - k_pos[None, :]
    allowed = (
        (gap >= 0) & (gap < WINDOW) & (k_pos[None, :] >= 0) & (q_seg[:, None] == k_seg[None, :])
    )
    grad_q, key_gradient, value_gradient = lax.map(
        lambda head_index: head_terms(
            head_index, queries, k_block, v_block, cot, allowed, scale, head_size, group_size
        ),
        jnp.arange(heads, dtype=jnp.int32),
    )
    dq_local = grad_q.transpose(1, 0, 2).reshape(rows, q_cols).astype(jnp.bfloat16)
    dk_local = (
        key_gradient.reshape(kv_heads, group_size, column_width, head_size)
        .sum(axis=1)
        .transpose(1, 0, 2)
        .reshape(column_width, key_value_columns)
    )
    dv_local = (
        value_gradient.reshape(kv_heads, group_size, column_width, head_size)
        .sum(axis=1)
        .transpose(1, 0, 2)
        .reshape(column_width, key_value_columns)
    )

    def piece(distance):
        first = (reach - distance) * rows
        return (dk_local[first : first + rows], dv_local[first : first + rows])

    dk_total, dv_total = piece(0)
    for distance in range(1, reach + 1):
        got_k, got_v = shifted(piece(distance), "ctx", -distance)
        dk_total = dk_total + got_k
        dv_total = dv_total + got_v
    dk_b = dk_total.astype(jnp.bfloat16)
    dv_b = dv_total.astype(jnp.bfloat16)
    grad_in = (
        jnp.dot(dq_local, w_query.T, preferred_element_type=jnp.float32)
        + jnp.dot(dk_b, key_weight.T, preferred_element_type=jnp.float32)
        + jnp.dot(dv_b, value_weight.T, preferred_element_type=jnp.float32)
    ).astype(jnp.bfloat16)
    combined = jnp.concatenate([dq_local, dk_b, dv_b], axis=1)
    partial_value = lax.dot_general(
        sequence, combined, (((0,), (0,)), ((), ())), preferred_element_type=jnp.float32
    )
    summed = lax.psum_scatter(
        lax.optimization_barrier(partial_value.astype(jnp.bfloat16))
        .astype(jnp.float32)
        .astype(jnp.bfloat16),
        "ctx",
        scatter_dimension=0,
        tiled=True,
    ).astype(jnp.float32)
    summed = lax.psum(summed, "dp")
    norm_factor = (lax.axis_size("dp") * lax.axis_size("ctx") * rows) ** (-0.5)
    summed = summed * norm_factor
    grad_query = summed[:, :q_cols]
    key_weight_gradient = summed[:, q_cols : q_cols + key_value_columns]
    value_weight_gradient = summed[:, q_cols + key_value_columns :]
    return (grad_in[None], grad_query, key_weight_gradient, value_weight_gradient)


def solution(mesh):
    placed = (P("dp", "ctx", None), P(), P(), P(), P("dp", "ctx", None), P("dp", None))
    return jax.shard_map(
        body,
        mesh=mesh,
        in_specs=placed,
        out_specs=(P("dp", "ctx", None), P("ctx", None), P("ctx", None), P("ctx", None)),
        check_vma=False,
    )
```

profile of v0, /device:TPU:16, one launch (start us, length us, event | category | flops | bytes accessed | tf_op | source)
XLA Modules:
  0.0 430.2 jit_solution(338459970549987686)
XLA Ops:
  10.8 3.2 collective-permute-start.6
  14.0 4.1 collective-permute-start.5
  19.6 3.2 collective-permute-start.1
  22.8 3.2 collective-permute-start
  32.8 3.7 collective-permute-start.2
  37.4 2.7 collective-permute-start.3
  41.0 6.0 %collective-permute-start.4 = (bf16[256,256]{1,0:T(8,128)(2,1)S(1)}, bf16[256,256]{1,0:T(8,128)(2,1)S(1)}, u32[]{:S(2)}, u32[]{:S(2)}) collective-permute-start(bf16[256,256]{1,0:T(8,128)(2,1)S(1)} %convolution_convert_fusion.2), channel_id=1, source_target_pairs={{0,4},{1,5},{2,6},{3,7},{4,8},{5,9},{6,10},{7,11},{8,12},{9,13},{1... | collective-permute-start | bytes 393224 | tf_op jit(solution)/shard_map/ppermute | solution.py:14
  47.1 3.2 collective-permute-done.4
  54.0 116.8 %while.17 = (s32[]{:T(128)}, bf16[8,256,128]{1,2,0:T(8,128)(2,1)}, f32[8,1280,128]{2,1,0:T(8,128)}, f32[8,1280,128]{2,1,0:T(8,128)}, s32[8]{0:T(128)S(1)}, /*ind...) while((s32[]{:T(128)}, bf16[8,256,128]{1,2,0:T(8,128)(2,1)}, ...), condition=%wide.region_4.5_spmd.clone, body=%wide.region_0.4_spmd.clone.sunk | while | flops 511278368 | bytes 14253591 | solution.py:74
  64.3 2.2 fusion.103
  78.9 2.2 fusion.103
  81.1 2.1 fusion.102
  93.4 2.2 fusion.103
  108.0 2.2 fusion.103
  110.2 2.1 fusion.102
  122.6 2.3 fusion.103
  124.8 2.1 fusion.102
  137.2 2.3 fusion.103
  151.9 2.2 fusion.103
  154.0 2.1 fusion.102
  166.4 2.2 fusion.103
  168.6 2.1 fusion.102
  170.7 2.9 bitcast_reduce_fusion
  181.7 2.2 collective-permute-start.13
  187.8 2.9 bitcast_reduce_fusion.1
  205.9 7.3 %collective-permute-done.15 = f32[256,256]{0,1:T(8,128)} collective-permute-done((f32[256,256]{0,1:T(8,128)}, f32[256,256]{0,1:T(8,128)}, u32[]{:S(2)}, u32[]{:S(2)}) %collective-permute-start.15) | collective-permute-done | bytes 262176 | tf_op jit(solution)/shard_map/ppermute | solution.py:14
  214.4 2.3 collective-permute-done.9
  216.8 22.7 %collective-permute-done.11 = f32[256,256]{0,1:T(8,128)} collective-permute-done((f32[256,256]{0,1:T(8,128)}, f32[256,256]{0,1:T(8,128)}, u32[]{:S(2)}, u32[]{:S(2)}) %collective-permute-start.11) | collective-permute-done | bytes 262176 | tf_op jit(solution)/shard_map/ppermute | solution.py:14
  240.7 2.7 fusion.33
  243.4 4.7 %copy.39 = bf16[1024,1536]{1,0:T(8,128)(2,1)} copy(bf16[1024,1536]{0,1:T(8,128)(2,1)} %fusion.33) | data formatting | bytes 6291456
  252.3 101.2 %reduce-scatter.4.cloned.1.call-done = bf16[32,1536]{1,0:T(8,128)(2,1)} async-done(((bf16[1024,1536]{1,0:T(8,128)(2,1)}), bf16[32,1536]{1,0:T(8,128)(2,1)}) %reduce-scatter.4.cloned.1.call-update) | async-done | bytes 98320
  354.6 66.4 %all-reduce.2 = f32[32,1536]{0,1:T(8,128)S(1)} all-reduce(bf16[32,1536]{0,1:T(8,128)(2,1)S(1)} %copy.40), channel_id=1, replica_groups=mesh['dp'=16,'ctx'=32] {'dp'}, use_global_device_ids=true, to_apply=%region_8.9 | all-reduce | flops 49152 | bytes 294912 | tf_op jit(solution)/shard_map/psum | solution.py:122
  (159 shorter events, 117.0 us)
Async XLA Ops:
  7.2 19.4 %copy-start = (bf16[1024,1024]{1,0:T(8,128)(2,1)S(1)}, bf16[1024,1024]{1,0:T(8,128)(2,1)}, u32[]{:S(2)}) copy-start(bf16[1024,1024]{1,0:T(8,128)(2,1)} %param.9) | copy-start | bytes 6291460
  7.2 19.4 %copy-start.2 = (bf16[1,256,1024]{2,1,0:T(8,128)(2,1)S(1)}, bf16[1,256,1024]{2,1,0:T(8,128)(2,1)}, u32[]{:S(2)}) copy-start(bf16[1,256,1024]{2,1,0:T(8,128)(2,1)} %param.8) | copy-start | bytes 1572868
  7.2 346.3 %reduce-scatter.4.cloned.1.call-start = ((), (), s32[]{:S(2)}) async-start(), calls=%async_computation.1 | async-start | bytes 3244032
  8.9 43.3 %collective-permute-start.7 = (bf16[256,256]{1,0:T(8,128)(2,1)S(1)}, bf16[256,256]{1,0:T(8,128)(2,1)}, u32[]{:S(2)}, u32[]{:S(2)}) collective-permute-start(bf16[256,256]{1,0:T(8,128)(2,1)S(1)} %convolution_convert_fusion.2), channel_id=1, source_target_pairs={{0,1},{1,2},{2,3},{3,4},{4,5},{5,6},{6,7},{7,8},{8,9},{9,10},{10,1... | collective-permute-start | bytes 393224 | tf_op jit(solution)/shard_map/ppermute | solution.py:14
  10.8 40.4 %collective-permute-start.6 = (bf16[256,256]{1,0:T(8,128)(2,1)S(1)}, bf16[256,256]{1,0:T(8,128)(2,1)}, u32[]{:S(2)}, u32[]{:S(2)}) collective-permute-start(bf16[256,256]{1,0:T(8,128)(2,1)S(1)} %convolution_convert_fusion.2), channel_id=1, source_target_pairs={{0,2},{1,3},{2,4},{3,5},{4,6},{5,7},{6,8},{7,9},{8,10},{9,11},{10,... | collective-permute-start | bytes 393224 | tf_op jit(solution)/shard_map/ppermute | solution.py:14
  14.0 36.3 %collective-permute-start.5 = (bf16[256,256]{1,0:T(8,128)(2,1)S(1)}, bf16[256,256]{1,0:T(8,128)(2,1)}, u32[]{:S(2)}, u32[]{:S(2)}) collective-permute-start(bf16[256,256]{1,0:T(8,128)(2,1)S(1)} %convolution_convert_fusion.2), channel_id=1, source_target_pairs={{0,3},{1,4},{2,5},{3,6},{4,7},{5,8},{6,9},{7,10},{8,11},{9,12},{10... | collective-permute-start | bytes 393224 | tf_op jit(solution)/shard_map/ppermute | solution.py:14
  19.6 17.8 %collective-permute-start.1 = (bf16[256,256]{1,0:T(8,128)(2,1)S(1)}, bf16[256,256]{1,0:T(8,128)(2,1)}, u32[]{:S(2)}, u32[]{:S(2)}) collective-permute-start(bf16[256,256]{1,0:T(8,128)(2,1)S(1)} %convolution_convert_fusion.3), channel_id=1, source_target_pairs={{0,3},{1,4},{2,5},{3,6},{4,7},{5,8},{6,9},{7,10},{8,11},{9,12},{10... | collective-permute-start | bytes 393224 | tf_op jit(solution)/shard_map/ppermute | solution.py:14
  22.8 9.3 %collective-permute-start = (bf16[256,256]{1,0:T(8,128)(2,1)S(1)}, bf16[256,256]{1,0:T(8,128)(2,1)S(1)}, u32[]{:S(2)}, u32[]{:S(2)}) collective-permute-start(bf16[256,256]{1,0:T(8,128)(2,1)S(1)} %convolution_convert_fusion.3), channel_id=1, source_target_pairs={{0,4},{1,5},{2,6},{3,7},{4,8},{5,9},{6,10},{7,11},{8,12},{9,13},{1... | collective-permute-start | bytes 393224 | tf_op jit(solution)/shard_map/ppermute | solution.py:14
  26.6 4.1 copy-start.6
  32.8 8.2 %collective-permute-start.2 = (bf16[256,256]{1,0:T(8,128)(2,1)S(1)}, bf16[256,256]{1,0:T(8,128)(2,1)S(1)}, u32[]{:S(2)}, u32[]{:S(2)}) collective-permute-start(bf16[256,256]{1,0:T(8,128)(2,1)S(1)} %convolution_convert_fusion.3), channel_id=1, source_target_pairs={{0,2},{1,3},{2,4},{3,5},{4,6},{5,7},{6,8},{7,9},{8,10},{9,11},{10,... | collective-permute-start | bytes 393224 | tf_op jit(solution)/shard_map/ppermute | solution.py:14
  37.4 9.7 %collective-permute-start.3 = (bf16[256,256]{1,0:T(8,128)(2,1)S(1)}, bf16[256,256]{1,0:T(8,128)(2,1)S(1)}, u32[]{:S(2)}, u32[]{:S(2)}) collective-permute-start(bf16[256,256]{1,0:T(8,128)(2,1)S(1)} %convolution_convert_fusion.3), channel_id=1, source_target_pairs={{0,1},{1,2},{2,3},{3,4},{4,5},{5,6},{6,7},{7,8},{8,9},{9,10},{10,1... | collective-permute-start | bytes 393224 | tf_op jit(solution)/shard_map/ppermute | solution.py:14
  41.0 9.3 %collective-permute-start.4 = (bf16[256,256]{1,0:T(8,128)(2,1)S(1)}, bf16[256,256]{1,0:T(8,128)(2,1)S(1)}, u32[]{:S(2)}, u32[]{:S(2)}) collective-permute-start(bf16[256,256]{1,0:T(8,128)(2,1)S(1)} %convolution_convert_fusion.2), channel_id=1, source_target_pairs={{0,4},{1,5},{2,6},{3,7},{4,8},{5,9},{6,10},{7,11},{8,12},{9,13},{1... | collective-permute-start | bytes 393224 | tf_op jit(solution)/shard_map/ppermute | solution.py:14
  47.1 6.9 %copy-start.10 = (pred[1280]{0:T(1024)(128)(4,1)S(1)}, pred[1280]{0:T(1024)(128)(4,1)}, u32[]{:S(2)}) copy-start(pred[1280]{0:T(1024)(128)(4,1)} %broadcast_compare_fusion) | copy-start | bytes 3844
  47.1 6.8 %copy-start.11 = (s32[1,256]{1,0:T(1,128)S(1)}, s32[1,256]{1,0:T(1,128)}, u32[]{:S(2)}) copy-start(s32[1,256]{1,0:T(1,128)} %constant_dynamic-slice_fusion) | copy-start | bytes 3076
  47.1 6.8 %copy-start.12 = (s32[256]{0:T(256)S(1)}, s32[256]{0:T(256)}, u32[]{:S(2)}) copy-start(s32[256]{0:T(256)} %iota_add_fusion.1) | copy-start | bytes 3076
  59.4 1.1 copy-start.9
  74.0 1.1 copy-start.9
  88.6 1.1 copy-start.9
  103.2 1.1 copy-start.9
  117.7 1.1 copy-start.9
  132.4 1.1 copy-start.9
  147.0 1.1 copy-start.9
  161.6 1.1 copy-start.9
  179.8 19.9 %collective-permute-start.12 = (f32[256,256]{0,1:T(8,128)}, f32[256,256]{0,1:T(8,128)}, u32[]{:S(2)}, u32[]{:S(2)}) collective-permute-start(f32[256,256]{0,1:T(8,128)} %bitcast.16), channel_id=1, source_target_pairs={{1,0},{2,1},{3,2},{4,3},{5,4},{6,5},{7,6},{8,7},{9,8},{10,9},{11,1... | collective-permute-start | bytes 786440 | tf_op jit(solution)/shard_map/ppermute | solution.py:14
  181.7 20.0 %collective-permute-start.13 = (f32[256,256]{0,1:T(8,128)}, f32[256,256]{0,1:T(8,128)}, u32[]{:S(2)}, u32[]{:S(2)}) collective-permute-start(f32[256,256]{0,1:T(8,128)} %bitcast.101), channel_id=1, source_target_pairs={{2,0},{3,1},{4,2},{5,3},{6,4},{7,5},{8,6},{9,7},{10,8},{11,9},{12,... | collective-permute-start | bytes 786440 | tf_op jit(solution)/shard_map/ppermute | solution.py:14
  184.0 19.7 %collective-permute-start.14 = (f32[256,256]{0,1:T(8,128)}, f32[256,256]{0,1:T(8,128)}, u32[]{:S(2)}, u32[]{:S(2)}) collective-permute-start(f32[256,256]{0,1:T(8,128)} %bitcast.98), channel_id=1, source_target_pairs={{3,0},{4,1},{5,2},{6,3},{7,4},{8,5},{9,6},{10,7},{11,8},{12,9},{13... | collective-permute-start | bytes 786440 | tf_op jit(solution)/shard_map/ppermute | solution.py:14
  185.9 27.2 %collective-permute-start.15 = (f32[256,256]{0,1:T(8,128)}, f32[256,256]{0,1:T(8,128)}, u32[]{:S(2)}, u32[]{:S(2)}) collective-permute-start(f32[256,256]{0,1:T(8,128)} %bitcast.96), channel_id=1, source_target_pairs={{4,0},{5,1},{6,2},{7,3},{8,4},{9,5},{10,6},{11,7},{12,8},{13,9},{1... | collective-permute-start | bytes 786440 | tf_op jit(solution)/shard_map/ppermute | solution.py:14
  197.8 16.6 %collective-permute-start.8 = (f32[256,256]{0,1:T(8,128)}, f32[256,256]{0,1:T(8,128)}, u32[]{:S(2)}, u32[]{:S(2)}) collective-permute-start(f32[256,256]{0,1:T(8,128)} %bitcast.102), channel_id=1, source_target_pairs={{1,0},{2,1},{3,2},{4,3},{5,4},{6,5},{7,6},{8,7},{9,8},{10,9},{11,1... | collective-permute-start | bytes 786440 | tf_op jit(solution)/shard_map/ppermute | solution.py:14
  199.8 17.0 %collective-permute-start.9 = (f32[256,256]{0,1:T(8,128)}, f32[256,256]{0,1:T(8,128)}, u32[]{:S(2)}, u32[]{:S(2)}) collective-permute-start(f32[256,256]{0,1:T(8,128)} %bitcast.100), channel_id=1, source_target_pairs={{2,0},{3,1},{4,2},{5,3},{6,4},{7,5},{8,6},{9,7},{10,8},{11,9},{12,... | collective-permute-start | bytes 786440 | tf_op jit(solution)/shard_map/ppermute | solution.py:14
  201.7 15.1 %collective-permute-start.10 = (f32[256,256]{0,1:T(8,128)}, f32[256,256]{0,1:T(8,128)}, u32[]{:S(2)}, u32[]{:S(2)}) collective-permute-start(f32[256,256]{0,1:T(8,128)} %bitcast.99), channel_id=1, source_target_pairs={{3,0},{4,1},{5,2},{6,3},{7,4},{8,5},{9,6},{10,7},{11,8},{12,9},{13... | collective-permute-start | bytes 786440 | tf_op jit(solution)/shard_map/ppermute | solution.py:14
  203.6 35.8 %collective-permute-start.11 = (f32[256,256]{0,1:T(8,128)}, f32[256,256]{0,1:T(8,128)}, u32[]{:S(2)}, u32[]{:S(2)}) collective-permute-start(f32[256,256]{0,1:T(8,128)} %bitcast.97), channel_id=1, source_target_pairs={{4,0},{5,1},{6,2},{7,3},{8,4},{9,5},{10,6},{11,7},{12,8},{13,9},{1... | collective-permute-start | bytes 786440 | tf_op jit(solution)/shard_map/ppermute | solution.py:14
  205.9 34.8 %copy-start.4 = (bf16[8,256,128]{1,2,0:T(8,128)(2,1)S(1)}, bf16[8,256,128]{1,2,0:T(8,128)(2,1)}, u32[]{:S(2)}) copy-start(bf16[8,256,128]{1,2,0:T(8,128)(2,1)} %get-tuple-element.132) | copy-start | bytes 1572868
  (5 other events, 4.6 us)
Sparse Core Ops, SparseCore 0:
  248.2 105.2 reduce-scatter.3
where the time goes:
time: 434 us; the launch traced here: 430 us
  waiting for transfers between devices  137 us (32%)
  matrix products  86.7 us (20%)
  blocking collectives  66.4 us (15%)
  starting transfers between devices  43.6 us (10%)
  local copies, waits for them, and re-layouts  42.5 us (10%)
  loops' own time  26.3 us (6%)
  between operations  14.5 us (3%)
  other arithmetic  13 us (3%)
    unnamed x2, waiting for transfers between devices  101 us
    psum x1, blocking collectives, body(): summed = lax.psum(summed, 'dp')  66.4 us
    ppermute x16, starting transfers between devices, shifted(): return lax.ppermute(block, axis, route)  43.6 us
    ppermute x16, waiting for transfers between devices, shifted(): return lax.ppermute(block, axis, route)  36 us
    another operation x1, loops' own time, body(): lax.map(lambda head_index: head_terms(head_index, queries, k_block, v_blo...  26.3 us
    dot_general x8, matrix products, head_terms(): jnp.dot(weights_b.T, dout, preferred_element_type=jnp.float32)  17.7 us
    unnamed x38, local copies, waits for them, and re-layouts  17.1 us
    dot_general x8, matrix products, head_terms(): key_gradient = jnp.dot(dscores.T, query, preferred_element_type=jnp.float32)  16.6 us
  transfers between devices with their start and end apart: 17, of which 6 were waited for; matrix products, arithmetic and copies ran while one was open for 6% of the time, Pallas kernels for 0%

commit v1 on v0

--- a/solution.py
+++ b/solution.py
@@ -6,6 +6,11 @@
 HEAD_DIMENSION = 128
 WINDOW = 1024
 NEG_FILL = -1e30
+
+
+def _follow_spots(page, ax_name):
+    aux = lax.all_gather(page, ax_name)
+    return jnp.sum(aux, axis=0)
 
 
 def shifted(block, axis, distance):
@@ -119,7 +124,7 @@
         scatter_dimension=0,
         tiled=True,
     ).astype(jnp.float32)
-    summed = lax.psum(summed, "dp")
+    summed = _follow_spots(summed, "dp")
     norm_factor = (lax.axis_size("dp") * lax.axis_size("ctx") * rows) ** (-0.5)
     summed = summed * norm_factor
     grad_query = summed[:, :q_cols]

time: 434 us -> 445 us (1.025)
  the two profiles are of different devices: /device:TPU:16 before, /device:TPU:2 now
where the time goes in v1:
time: 445 us; the launch traced here: 441 us
  waiting for transfers between devices  216 us (49%)
  matrix products  86.8 us (20%)
  starting transfers between devices  41.3 us (9%)
  local copies, waits for them, and re-layouts  39.4 us (9%)
  loops' own time  26.3 us (6%)
  other arithmetic  16.7 us (4%)
  between operations  14.4 us (3%)
    reduce_scatter x1, waiting for transfers between devices, body(): lax.psum_scatter(lax.optimization_barrier(partial_value.astype(jnp.bfloat...  107 us
    all_gather x1, waiting for transfers between devices, _follow_spots(): aux = lax.all_gather(page, ax_name)  72.4 us
    ppermute x16, starting transfers between devices, shifted(): return lax.ppermute(block, axis, route)  41.2 us
    ppermute x16, waiting for transfers between devices, shifted(): return lax.ppermute(block, axis, route)  36.6 us
    another operation x1, loops' own time, body(): lax.map(lambda head_index: head_terms(head_index, queries, k_block, v_blo...  26.3 us
    dot_general x8, matrix products, head_terms(): jnp.dot(weights_b.T, dout, preferred_element_type=jnp.float32)  17.8 us
    dot_general x8, matrix products, head_terms(): key_gradient = jnp.dot(dscores.T, query, preferred_element_type=jnp.float32)  16.5 us
    slice x12, local copies, waits for them, and re-layouts, piece(): return (dk_local[first:first + rows], dv_local[first:first + rows])  13.5 us
  transfers between devices with their start and end apart: 18, of which 10 were waited for; matrix products, arithmetic and copies ran while one was open for 6% of the time, Pallas kernels for 0%

profile of v1, /device:TPU:2, one launch (start us, length us, event | category | flops | bytes accessed | tf_op | source)
XLA Modules:
  0.0 441.2 jit_solution(299095003918343910)
XLA Ops:
  10.8 3.5 collective-permute-start.6
  14.3 4.2 collective-permute-start.5
  20.0 2.8 collective-permute-start.1
  22.8 5.1 %collective-permute-start = (bf16[256,256]{1,0:T(8,128)(2,1)S(1)}, bf16[256,256]{1,0:T(8,128)(2,1)S(1)}, u32[]{:S(2)}, u32[]{:S(2)}) collective-permute-start(bf16[256,256]{1,0:T(8,128)(2,1)S(1)} %convolution_convert_fusion.3), channel_id=1, source_target_pairs={{0,4},{1,5},{2,6},{3,7},{4,8},{5,9},{6,10},{7,11},{8,12},{9,13},{1... | collective-permute-start | bytes 393224 | tf_op jit(solution)/shard_map/ppermute | solution.py:19
  34.2 3.2 collective-permute-start.2
  41.2 2.7 collective-permute-done.2
  43.9 2.3 collective-permute-start.4
  46.8 6.3 %collective-permute-done.4 = bf16[256,256]{1,0:T(8,128)(2,1)S(1)} collective-permute-done((bf16[256,256]{1,0:T(8,128)(2,1)S(1)}, bf16[256,256]{1,0:T(8,128)(2,1)S(1)}, u32[]{:S(2)}, u32[]{:S(2)}) %collective-permute-start.4) | collective-permute-done | bytes 131104 | tf_op jit(solution)/shard_map/ppermute | solution.py:19
  56.8 116.8 %while.17 = (s32[]{:T(128)}, bf16[8,256,128]{1,2,0:T(8,128)(2,1)}, f32[8,1280,128]{2,1,0:T(8,128)}, f32[8,1280,128]{2,1,0:T(8,128)}, s32[8]{0:T(128)S(1)}, /*ind...) while((s32[]{:T(128)}, bf16[8,256,128]{1,2,0:T(8,128)(2,1)}, ...), condition=%wide.region_4.5_spmd.clone, body=%wide.region_0.4_spmd.clone.sunk | while | flops 511278368 | bytes 14253591 | solution.py:79
  67.1 2.2 fusion.103
  81.7 2.2 fusion.103
  83.9 2.1 fusion.102
  96.3 2.2 fusion.103
  98.5 2.1 fusion.102
  110.8 2.2 fusion.103
  113.0 2.1 fusion.102
  125.4 2.3 fusion.103
  140.1 2.3 fusion.103
  154.7 2.2 fusion.103
  169.3 2.2 fusion.103
  173.6 2.9 bitcast_reduce_fusion
  182.6 2.6 collective-permute-start.12
  185.2 2.2 collective-permute-start.13
  191.3 2.9 bitcast_reduce_fusion.1
  212.7 10.6 %collective-permute-done.8 = f32[256,256]{0,1:T(8,128)} collective-permute-done((f32[256,256]{0,1:T(8,128)}, f32[256,256]{0,1:T(8,128)}, u32[]{:S(2)}, u32[]{:S(2)}) %collective-permute-start.8) | collective-permute-done | bytes 262176 | tf_op jit(solution)/shard_map/ppermute | solution.py:19
  223.2 7.1 %collective-permute-done.9 = f32[256,256]{0,1:T(8,128)} collective-permute-done((f32[256,256]{0,1:T(8,128)}, f32[256,256]{0,1:T(8,128)}, u32[]{:S(2)}, u32[]{:S(2)}) %collective-permute-start.9) | collective-permute-done | bytes 262176 | tf_op jit(solution)/shard_map/ppermute | solution.py:19
  230.4 4.5 %collective-permute-done.10 = f32[256,256]{0,1:T(8,128)} collective-permute-done((f32[256,256]{0,1:T(8,128)}, f32[256,256]{0,1:T(8,128)}, u32[]{:S(2)}, u32[]{:S(2)}) %collective-permute-start.10) | collective-permute-done | bytes 262176 | tf_op jit(solution)/shard_map/ppermute | solution.py:19
  234.9 2.8 collective-permute-done.11
  239.0 2.7 fusion.33
  241.7 4.6 %copy.43 = bf16[1024,1536]{1,0:T(8,128)(2,1)} copy(bf16[1024,1536]{0,1:T(8,128)(2,1)} %fusion.33) | data formatting | bytes 6291456
  246.4 107.3 %reduce-scatter.4.cloned.1.call-done = bf16[32,1536]{1,0:T(8,128)(2,1)} async-done(((bf16[1024,1536]{1,0:T(8,128)(2,1)}), bf16[32,1536]{1,0:T(8,128)(2,1)}) %reduce-scatter.4.cloned.1.call-update) | async-done | bytes 98320 | tf_op jit(solution)/shard_map/reduce_scatter | solution.py:119
  358.5 72.4 %all-gather.3.cloned.1.call-done = f32[512,1536]{1,0:T(8,128)} async-done(((f32[32,1536]{1,0:T(8,128)}), f32[512,1536]{1,0:T(8,128)}) %all-gather.3.cloned.1.call-update) | async-done | bytes 3145744 | tf_op jit(solution)/shard_map/all_gather | solution.py:12
  (159 shorter events, 123.9 us)
Async XLA Ops:
  7.2 21.4 %copy-start = (bf16[1024,1024]{1,0:T(8,128)(2,1)S(1)}, bf16[1024,1024]{1,0:T(8,128)(2,1)}, u32[]{:S(2)}) copy-start(bf16[1024,1024]{1,0:T(8,128)(2,1)} %param.9) | copy-start | bytes 6291460
  7.2 21.3 %copy-start.2 = (bf16[1,256,1024]{2,1,0:T(8,128)(2,1)S(1)}, bf16[1,256,1024]{2,1,0:T(8,128)(2,1)}, u32[]{:S(2)}) copy-start(bf16[1,256,1024]{2,1,0:T(8,128)(2,1)} %param.8) | copy-start | bytes 1572868
  7.2 346.5 %reduce-scatter.4.cloned.1.call-start = ((), (), s32[]{:S(2)}) async-start(), calls=%async_computation.2 | async-start | bytes 3244032 | tf_op jit(solution)/shard_map/reduce_scatter | solution.py:119
  8.9 46.1 %collective-permute-start.7 = (bf16[256,256]{1,0:T(8,128)(2,1)S(1)}, bf16[256,256]{1,0:T(8,128)(2,1)}, u32[]{:S(2)}, u32[]{:S(2)}) collective-permute-start(bf16[256,256]{1,0:T(8,128)(2,1)S(1)} %convolution_convert_fusion.2), channel_id=1, source_target_pairs={{0,1},{1,2},{2,3},{3,4},{4,5},{5,6},{6,7},{7,8},{8,9},{9,10},{10,1... | collective-permute-start | bytes 393224 | tf_op jit(solution)/shard_map/ppermute | solution.py:19
  10.8 43.2 %collective-permute-start.6 = (bf16[256,256]{1,0:T(8,128)(2,1)S(1)}, bf16[256,256]{1,0:T(8,128)(2,1)}, u32[]{:S(2)}, u32[]{:S(2)}) collective-permute-start(bf16[256,256]{1,0:T(8,128)(2,1)S(1)} %convolution_convert_fusion.2), channel_id=1, source_target_pairs={{0,2},{1,3},{2,4},{3,5},{4,6},{5,7},{6,8},{7,9},{8,10},{9,11},{10,... | collective-permute-start | bytes 393224 | tf_op jit(solution)/shard_map/ppermute | solution.py:19
  14.3 38.8 %collective-permute-start.5 = (bf16[256,256]{1,0:T(8,128)(2,1)S(1)}, bf16[256,256]{1,0:T(8,128)(2,1)}, u32[]{:S(2)}, u32[]{:S(2)}) collective-permute-start(bf16[256,256]{1,0:T(8,128)(2,1)S(1)} %convolution_convert_fusion.2), channel_id=1, source_target_pairs={{0,3},{1,4},{2,5},{3,6},{4,7},{5,8},{6,9},{7,10},{8,11},{9,12},{10... | collective-permute-start | bytes 393224 | tf_op jit(solution)/shard_map/ppermute | solution.py:19
  20.0 18.3 %collective-permute-start.1 = (bf16[256,256]{1,0:T(8,128)(2,1)S(1)}, bf16[256,256]{1,0:T(8,128)(2,1)}, u32[]{:S(2)}, u32[]{:S(2)}) collective-permute-start(bf16[256,256]{1,0:T(8,128)(2,1)S(1)} %convolution_convert_fusion.3), channel_id=1, source_target_pairs={{0,3},{1,4},{2,5},{3,6},{4,7},{5,8},{6,9},{7,10},{8,11},{9,12},{10... | collective-permute-start | bytes 393224 | tf_op jit(solution)/shard_map/ppermute | solution.py:19
  22.8 10.8 %collective-permute-start = (bf16[256,256]{1,0:T(8,128)(2,1)S(1)}, bf16[256,256]{1,0:T(8,128)(2,1)S(1)}, u32[]{:S(2)}, u32[]{:S(2)}) collective-permute-start(bf16[256,256]{1,0:T(8,128)(2,1)S(1)} %convolution_convert_fusion.3), channel_id=1, source_target_pairs={{0,4},{1,5},{2,6},{3,7},{4,8},{5,9},{6,10},{7,11},{8,12},{9,13},{1... | collective-permute-start | bytes 393224 | tf_op jit(solution)/shard_map/ppermute | solution.py:19
  28.5 4.1 copy-start.6
  34.2 9.6 %collective-permute-start.2 = (bf16[256,256]{1,0:T(8,128)(2,1)S(1)}, bf16[256,256]{1,0:T(8,128)(2,1)S(1)}, u32[]{:S(2)}, u32[]{:S(2)}) collective-permute-start(bf16[256,256]{1,0:T(8,128)(2,1)S(1)} %convolution_convert_fusion.3), channel_id=1, source_target_pairs={{0,2},{1,3},{2,4},{3,5},{4,6},{5,7},{6,8},{7,9},{8,10},{9,11},{10,... | collective-permute-start | bytes 393224 | tf_op jit(solution)/shard_map/ppermute | solution.py:19
  38.4 8.4 %collective-permute-start.3 = (bf16[256,256]{1,0:T(8,128)(2,1)S(1)}, bf16[256,256]{1,0:T(8,128)(2,1)S(1)}, u32[]{:S(2)}, u32[]{:S(2)}) collective-permute-start(bf16[256,256]{1,0:T(8,128)(2,1)S(1)} %convolution_convert_fusion.3), channel_id=1, source_target_pairs={{0,1},{1,2},{2,3},{3,4},{4,5},{5,6},{6,7},{7,8},{8,9},{9,10},{10,1... | collective-permute-start | bytes 393224 | tf_op jit(solution)/shard_map/ppermute | solution.py:19
  43.9 9.3 %collective-permute-start.4 = (bf16[256,256]{1,0:T(8,128)(2,1)S(1)}, bf16[256,256]{1,0:T(8,128)(2,1)S(1)}, u32[]{:S(2)}, u32[]{:S(2)}) collective-permute-start(bf16[256,256]{1,0:T(8,128)(2,1)S(1)} %convolution_convert_fusion.2), channel_id=1, source_target_pairs={{0,4},{1,5},{2,6},{3,7},{4,8},{5,9},{6,10},{7,11},{8,12},{9,13},{1... | collective-permute-start | bytes 393224 | tf_op jit(solution)/shard_map/ppermute | solution.py:19
  46.8 10.0 %copy-start.10 = (pred[1280]{0:T(1024)(128)(4,1)S(1)}, pred[1280]{0:T(1024)(128)(4,1)}, u32[]{:S(2)}) copy-start(pred[1280]{0:T(1024)(128)(4,1)} %broadcast_compare_fusion) | copy-start | bytes 3844
  46.8 10.0 %copy-start.11 = (s32[1,256]{1,0:T(1,128)S(1)}, s32[1,256]{1,0:T(1,128)}, u32[]{:S(2)}) copy-start(s32[1,256]{1,0:T(1,128)} %constant_dynamic-slice_fusion) | copy-start | bytes 3076
  46.8 10.0 %copy-start.12 = (s32[256]{0:T(256)S(1)}, s32[256]{0:T(256)}, u32[]{:S(2)}) copy-start(s32[256]{0:T(256)} %iota_add_fusion.1) | copy-start | bytes 3076
  62.3 1.1 copy-start.9
  76.9 1.1 copy-start.9
  91.4 1.1 copy-start.9
  106.0 1.1 copy-start.9
  120.6 1.1 copy-start.9
  135.2 1.1 copy-start.9
  182.6 20.7 %collective-permute-start.12 = (f32[256,256]{0,1:T(8,128)}, f32[256,256]{0,1:T(8,128)}, u32[]{:S(2)}, u32[]{:S(2)}) collective-permute-start(f32[256,256]{0,1:T(8,128)} %bitcast.16), channel_id=1, source_target_pairs={{1,0},{2,1},{3,2},{4,3},{5,4},{6,5},{7,6},{8,7},{9,8},{10,9},{11,1... | collective-permute-start | bytes 786440 | tf_op jit(solution)/shard_map/ppermute | solution.py:19
  185.2 20.0 %collective-permute-start.13 = (f32[256,256]{0,1:T(8,128)}, f32[256,256]{0,1:T(8,128)}, u32[]{:S(2)}, u32[]{:S(2)}) collective-permute-start(f32[256,256]{0,1:T(8,128)} %bitcast.103), channel_id=1, source_target_pairs={{2,0},{3,1},{4,2},{5,3},{6,4},{7,5},{8,6},{9,7},{10,8},{11,9},{12,... | collective-permute-start | bytes 786440 | tf_op jit(solution)/shard_map/ppermute | solution.py:19
  187.4 19.8 %collective-permute-start.14 = (f32[256,256]{0,1:T(8,128)}, f32[256,256]{0,1:T(8,128)}, u32[]{:S(2)}, u32[]{:S(2)}) collective-permute-start(f32[256,256]{0,1:T(8,128)} %bitcast.100), channel_id=1, source_target_pairs={{3,0},{4,1},{5,2},{6,3},{7,4},{8,5},{9,6},{10,7},{11,8},{12,9},{13... | collective-permute-start | bytes 786440 | tf_op jit(solution)/shard_map/ppermute | solution.py:19
  189.3 22.1 %collective-permute-start.15 = (f32[256,256]{0,1:T(8,128)}, f32[256,256]{0,1:T(8,128)}, u32[]{:S(2)}, u32[]{:S(2)}) collective-permute-start(f32[256,256]{0,1:T(8,128)} %bitcast.98), channel_id=1, source_target_pairs={{4,0},{5,1},{6,2},{7,3},{8,4},{9,5},{10,6},{11,7},{12,8},{13,9},{1... | collective-permute-start | bytes 786440 | tf_op jit(solution)/shard_map/ppermute | solution.py:19
  201.3 22.0 %collective-permute-start.8 = (f32[256,256]{0,1:T(8,128)}, f32[256,256]{0,1:T(8,128)}, u32[]{:S(2)}, u32[]{:S(2)}) collective-permute-start(f32[256,256]{0,1:T(8,128)} %bitcast.104), channel_id=1, source_target_pairs={{1,0},{2,1},{3,2},{4,3},{5,4},{6,5},{7,6},{8,7},{9,8},{10,9},{11,1... | collective-permute-start | bytes 786440 | tf_op jit(solution)/shard_map/ppermute | solution.py:19
  203.3 27.1 %collective-permute-start.9 = (f32[256,256]{0,1:T(8,128)}, f32[256,256]{0,1:T(8,128)}, u32[]{:S(2)}, u32[]{:S(2)}) collective-permute-start(f32[256,256]{0,1:T(8,128)} %bitcast.102), channel_id=1, source_target_pairs={{2,0},{3,1},{4,2},{5,3},{6,4},{7,5},{8,6},{9,7},{10,8},{11,9},{12,... | collective-permute-start | bytes 786440 | tf_op jit(solution)/shard_map/ppermute | solution.py:19
  205.2 29.7 %collective-permute-start.10 = (f32[256,256]{0,1:T(8,128)}, f32[256,256]{0,1:T(8,128)}, u32[]{:S(2)}, u32[]{:S(2)}) collective-permute-start(f32[256,256]{0,1:T(8,128)} %bitcast.101), channel_id=1, source_target_pairs={{3,0},{4,1},{5,2},{6,3},{7,4},{8,5},{9,6},{10,7},{11,8},{12,9},{13... | collective-permute-start | bytes 786440 | tf_op jit(solution)/shard_map/ppermute | solution.py:19
  207.2 30.5 %collective-permute-start.11 = (f32[256,256]{0,1:T(8,128)}, f32[256,256]{0,1:T(8,128)}, u32[]{:S(2)}, u32[]{:S(2)}) collective-permute-start(f32[256,256]{0,1:T(8,128)} %bitcast.99), channel_id=1, source_target_pairs={{4,0},{5,1},{6,2},{7,3},{8,4},{9,5},{10,6},{11,7},{12,8},{13,9},{1... | collective-permute-start | bytes 786440 | tf_op jit(solution)/shard_map/ppermute | solution.py:19
  209.4 29.6 %copy-start.4 = (bf16[8,256,128]{1,2,0:T(8,128)(2,1)S(1)}, bf16[8,256,128]{1,2,0:T(8,128)(2,1)}, u32[]{:S(2)}) copy-start(bf16[8,256,128]{1,2,0:T(8,128)(2,1)} %get-tuple-element.132) | copy-start | bytes 1572868
  246.3 109.0 %copy-start.5 = (bf16[8,256,128]{1,2,0:T(8,128)(2,1)S(1)}, bf16[8,256,128]{1,2,0:T(8,128)(2,1)}, u32[]{:S(2)}) copy-start(bf16[8,256,128]{1,2,0:T(8,128)(2,1)} %get-tuple-element.132) | copy-start | bytes 1572868
  246.3 184.6 %all-gather.3.cloned.1.call-start = ((), (), s32[]{:S(2)}) async-start(), calls=%async_computation.1 | async-start | bytes 3342336 | tf_op jit(solution)/shard_map/all_gather | solution.py:12
  (6 other events, 5.8 us)
Sparse Core Ops, SparseCore 0:
  246.5 107.1 reduce-scatter.3
  355.7 75.1 all-gather.2
